TPU v7x, 256 devices: a whole 4x4x8 slice. The times are simulated.
256 devices in a mesh: sec: 16 (over x, y_hi, core), span: 16 (over z, y_lo).
Axes of the slice: x: 4, y: 4 (y_hi: 2, y_lo: 2; y = y_hi * 2 + y_lo), z: 8, core: 2. Of those that a mesh axis runs over, the one named last changes fastest.
Arguments:
- density: float32 [384, 4096], P('sec', 'span'), may hold values from 0.5 to 2
- fields: float32 [4, 384, 4096], P(None, 'sec', 'span'), may hold values from -6 to 6
- bins: int32 [384, 4096], P('sec', 'span'), may hold values from 0 to 127
- owner: int32 [384], P('sec'), may hold values from 0 to 255
- species: float32 [256, 32, 128], P(('sec', 'span')), may hold values from -6 to 6
- rate_matrix: float32 [32, 32], replicated, may hold values from -1 to 1
- inv_weight: float32 [32], replicated, may hold values from 0.5 to 2
- formation: float32 [32], replicated, may hold values from -4 to 4
Outputs:
- species_out: float32 [256, 32, 128], P(('sec', 'span'))
- density_out: float32 [384, 4096], P('sec', 'span')
- fields_out: float32 [4, 384, 4096], P(None, 'sec', 'span')
All inputs are finite; a program needn't handle non-finite values.
Results may differ from a plain program's by a relative error of at most 0.0003.
Values sent between devices are 32-bit elements; how exact they have to be, the bound alone decides.
No kernel may reach another device: no remote copies, remote signals or barrier semaphores. Data moves between devices by JAX's collectives and lax.ppermute only.
A program may use at most 64 MiB of HBM per device.

v0:
```python
import math
import jax
import jax.numpy as jnp
from jax import lax
from jax.sharding import PartitionSpec as P

COUPLING = 2


def from_behind(value, axis, steps):
    count = lax.axis_size(axis)
    first, last = (max(0, -steps), min(count, count - steps))
    return lax.ppermute(value, axis, [(source, source + steps) for source in range(first, last)])


def extended_2(shard, sides, width):
    for axis, dim in sides:
        count, length = (lax.axis_size(axis), shard.shape[dim])
        up = [(i, (i + 1) % count) for i in range(count)]
        down = [(j, i) for i, j in up]
        last = lax.slice_in_dim(shard, length - width, length, axis=dim)
        first = lax.slice_in_dim(shard, 0, width, axis=dim)
        before = lax.ppermute(last, axis, up)
        after = lax.ppermute(first, axis, down)
        shard = jnp.concatenate([before, shard, after], axis=dim)
    return shard


def column_sums(values, bins, nbins):
    cols, quant, zlen = values.shape
    block = math.gcd(cols, 16)
    value_blocks = values.reshape(cols // block, block, quant, zlen)
    bin_blocks = bins.reshape(cols // block, block, zlen)

    def one_block(pair):
        vals, labels = pair
        hot = (labels[:, :, None] == jnp.arange(nbins, dtype=jnp.int32)).astype(jnp.float32)
        return jnp.einsum("cqz,czb->cqb", vals, hot, precision=lax.Precision.HIGHEST)

    out = lax.map(one_block, (value_blocks, bin_blocks))
    return out.reshape(cols, quant * nbins)


def body(density, fields, bins, owner, species, rate_matrix, inv_weight, formation):
    nbins = species.shape[2]
    nspec = species.shape[1]
    sections = lax.axis_size("sec") * lax.axis_size("span")
    mine = lax.axis_index("sec") * lax.axis_size("span") + lax.axis_index("span")
    eta = (jnp.arange(nbins, dtype=jnp.float32) + 0.5) / nbins
    index = owner[:, None] * nbins + bins
    for step in range(COUPLING):
        values = jnp.stack([density] + [density * fields[k] for k in range(4)], axis=1)
        hist = column_sums(values, bins, nbins)
        hot = (owner[:, None] == jnp.arange(sections, dtype=jnp.int32)[None, :]).astype(jnp.float32)
        total = lax.psum(
            lax.dot_general(
                hot,
                hist,
                (((0,), (0,)), ((), ())),
                precision=lax.Precision.HIGHEST,
                preferred_element_type=jnp.float32,
            ),
            ("sec", "span"),
        )
        own = lax.dynamic_slice_in_dim(total, mine, 1, 0)
        own = own.reshape(5, nbins)
        weight = jnp.maximum(own[0], 1.0)
        cond = own[1:] / weight[None]
        current = species[0]
        before = from_behind(species, ("sec", "span"), 1)[0]
        temp = 1.0 + 4.0 * eta * (1.0 - eta) + 0.5 * jnp.tanh(cond[2])
        rate = jnp.exp(2.0 * (1.0 - 1.0 / temp))
        react = (
            jnp.dot(
                rate_matrix,
                current,
                precision=lax.Precision.HIGHEST,
                preferred_element_type=jnp.float32,
            )
            * rate[None, :]
        )
        padded = jnp.pad(current, ((0, 0), (1, 1)))
        lap = padded[:, 2:] + padded[:, :-2] - 2.0 * current
        mixing = 0.2 * jax.nn.sigmoid(cond[1])
        carried = 0.3 * jax.nn.sigmoid(cond[0])
        updated = (
            current + mixing[None, :] * lap - carried[None, :] * (current - before) + 0.2 * react
        )
        species = updated[None]
        mix = 1.0 + jnp.sum(inv_weight[:, None] * updated * updated, axis=0) / nspec
        rho_c = 1.0 / (temp * mix)
        temp_c = (
            temp
            + 0.1 * jnp.sum(formation[:, None] * react, axis=0)
            - 0.2 * jax.nn.sigmoid(cond[3]) * (temp - 0.5)
        )
        table = jnp.stack([rho_c, temp_c])[None]
        whole = lax.all_gather(table, ("sec", "span"), axis=0, tiled=True)
        rho_cell = whole[:, 0, :].reshape(-1)[index]
        temp_cell = whole[:, 1, :].reshape(-1)[index]
        extended = extended_2(fields, (("span", 2),), 1)
        lapz = extended[:, :, 2:] + extended[:, :, :-2] - 2.0 * fields
        fields = fields + 0.2 * lapz
        fields = fields.at[2].add(0.3 * (temp_cell - fields[2]))
        density = rho_cell
    return (species, density, fields)


def solution(mesh):
    return jax.shard_map(
        body,
        mesh=mesh,
        in_specs=(
            P("sec", "span"),
            P(None, "sec", "span"),
            P("sec", "span"),
            P("sec"),
            P(("sec", "span"), None, None),
            P(),
            P(),
            P(),
        ),
        out_specs=(P(("sec", "span"), None, None), P("sec", "span"), P(None, "sec", "span")),
        check_vma=False,
    )
```

profile of v0, /device:TPU:0, one launch (start us, length us, event | category | flops | bytes accessed | tf_op | source)
XLA Modules:
  0.0 1920.2 jit_solution(5151774485042406274)
XLA Ops:
  7.2 0.8 stack.38
  8.1 0.8 bitcast_multiply_fusion
  10.0 2.4 while.22
  10.8 0.8 fusion.68
  11.6 0.8 fusion.68
  13.1 1.4 fusion.21
  15.2 1.8 collective-permute-start
  17.0 5.3 collective-permute-start.1
  22.5 1.6 collective-permute-done.1
  24.1 4.4 collective-permute-done.2
  28.7 242.0 %all-reduce.5.cloned.1.call-done = f32[256,640]{1,0:T(8,128)} async-done(((f32[256,640]{1,0:T(8,128)}), f32[256,640]{1,0:T(8,128)}) %all-reduce.5.cloned.1.call-update) | async-done | bytes 655376 | tf_op jit(solution)/shard_map/psum | solution.py:55
  273.1 624.5 %all-gather.2 = f32[256,2,128]{2,1,0:T(2,128)S(1)} all-gather(f32[1,2,128]{2,1,0:T(2,128)S(1)} %maximum_bitcast_fusion), channel_id=2, replica_groups=mesh['sec'=16,'span'=16] {'sec','span'}, dimensions={0}, use_global_device_ids=true | all-gather | bytes 263168 | tf_op jit(solution)/shard_map/all_gather | solution.py:98
  897.8 34.3 %gather_fusion.1 = f32[6144]{0:T(1024)S(1)} fusion(f32[32768]{0:T(1024)S(1)} %bitcast.132, s32[6144]{0:T(1024)S(1)} %broadcast_clamp_fusion), kind=kCustom, calls=%fused_computation.1 | custom fusion | bytes 73728 | tf_op jit(solution)/shard_map/gather | solution.py:100
  932.1 34.3 %gather_fusion = f32[6144]{0:T(1024)S(1)} fusion(f32[32768]{0:T(1024)S(1)} %bitcast.130, s32[6144]{0:T(1024)S(1)} %broadcast_clamp_fusion), kind=kCustom, calls=%fused_computation | custom fusion | bytes 73728 | tf_op jit(solution)/shard_map/gather | solution.py:99
  966.7 2.5 while.23
  966.7 0.8 fusion.70
  969.2 1.4 fusion.18
  970.8 2.0 collective-permute-start.5
  972.8 1.9 collective-permute-start.3
  975.0 2.1 collective-permute-done.5
  977.2 239.2 %all-reduce.7.cloned.1.call-done = f32[256,640]{1,0:T(8,128)} async-done(((f32[256,640]{1,0:T(8,128)}), f32[256,640]{1,0:T(8,128)}) %all-reduce.7.cloned.1.call-update) | async-done | bytes 655376 | tf_op jit(solution)/shard_map/psum | solution.py:55
  1218.8 624.5 %all-gather.3 = f32[256,2,128]{2,1,0:T(2,128)S(1)} all-gather(f32[1,2,128]{2,1,0:T(2,128)S(1)} %maximum_bitcast_fusion.1), channel_id=3, replica_groups=mesh['sec'=16,'span'=16] {'sec','span'}, dimensions={0}, use_global_device_ids=true | all-gather | bytes 263168 | tf_op jit(solution)/shard_map/all_gather | solution.py:98
  1843.5 34.3 %gather_fusion.3 = f32[6144]{0:T(1024)S(1)} fusion(f32[32768]{0:T(1024)S(1)} %bitcast.133, s32[6144]{0:T(1024)S(1)} %broadcast_clamp_fusion), kind=kCustom, calls=%fused_computation.3 | custom fusion | bytes 73728 | tf_op jit(solution)/shard_map/gather | solution.py:100
  1877.8 34.3 %gather_fusion.2 = f32[6144]{0:T(1024)S(1)} fusion(f32[32768]{0:T(1024)S(1)} %bitcast.131, s32[6144]{0:T(1024)S(1)} %broadcast_clamp_fusion), kind=kCustom, calls=%fused_computation.2 | custom fusion | bytes 73728 | tf_op jit(solution)/shard_map/gather | solution.py:99
  (76 shorter events, 12.4 us)
Async XLA Ops:
  7.2 265.1 %copy-start = (f32[32,32]{1,0:T(8,128)S(1)}, f32[32,32]{1,0:T(8,128)}, u32[]{:S(2)}) copy-start(f32[32,32]{1,0:T(8,128)} %param.21) | copy-start | bytes 12292
  7.2 263.5 %all-reduce.5.cloned.1.call-start = ((), (), s32[]{:S(2)}) async-start(), calls=%async_computation | async-start | bytes 1310720 | tf_op jit(solution)/shard_map/psum | solution.py:55
  7.2 0.8 copy-start.4
  9.2 0.7 copy-start.2
  12.4 0.7 copy-start.5
  14.5 0.7 copy-start.7
  14.5 2.5 copy-start.1
  14.5 1201.9 %all-reduce.7.cloned.1.call-start = ((), (), s32[]{:S(2)}) async-start(), calls=%async_computation.1 | async-start | bytes 1310720 | tf_op jit(solution)/shard_map/psum | solution.py:55
  15.2 257.0 %collective-permute-start = (f32[1,32,128]{2,1,0:T(8,128)S(1)}, f32[1,32,128]{2,1,0:T(8,128)S(1)}, u32[]{:S(2)}, u32[]{:S(2)}) collective-permute-start(f32[1,32,128]{2,1,0:T(8,128)S(1)} %copy-done.7), channel_id=1, source_target_pairs={{0,1},{1,2},{2,3},{3,4},{4,5},{5,6},{6,7},{7,8},{8,9},{9,10},{10,1... | collective-permute-start | bytes 49160 | tf_op jit(solution)/shard_map/ppermute | solution.py:13
  17.0 7.1 collective-permute-start.1
  22.4 6.2 collective-permute-start.2
  272.2 0.7 copy-start.6
  272.2 0.7 copy-start.8
  970.7 4.2 collective-permute-start.4
  970.8 6.3 collective-permute-start.5
  972.8 245.3 %collective-permute-start.3 = (f32[1,32,128]{2,1,0:T(8,128)S(1)}, f32[1,32,128]{2,1,0:T(8,128)S(1)}, u32[]{:S(2)}, u32[]{:S(2)}) collective-permute-start(f32[1,32,128]{2,1,0:T(8,128)S(1)} %bitcast.139), channel_id=1, source_target_pairs={{0,1},{1,2},{2,3},{3,4},{4,5},{5,6},{6,7},{7,8},{8,9},{9,10},{10,1... | collective-permute-start | bytes 49160 | tf_op jit(solution)/shard_map/ppermute | solution.py:13
  1912.7 0.6 copy-start.3
Sparse Core Ops, SparseCore 0:
  14.6 256.0 all-reduce.4
  970.8 245.5 all-reduce.6
where the time goes:
time: 1920 us
  blocking collectives  1250 us (65%)
  waiting for transfers between devices  490 us (26%)
  local copies, waits for them, and re-layouts  145 us (8%)
    all_gather x2, blocking collectives, body(): whole = lax.all_gather(table, ('sec', 'span'), axis=0, tiled=True)  1250 us
    psum x2, waiting for transfers between devices, body(): lax.psum(lax.dot_general(hot, hist, (((0,), (0,)), ((), ())), precision=l...  481 us
    gather x3, local copies, waits for them, and re-layouts, body(): rho_cell = whole[:, 0, :].reshape(-1)[index]  69.2 us
    gather x4, local copies, waits for them, and re-layouts, body(): temp_cell = whole[:, 1, :].reshape(-1)[index]  68.6 us
  transfers between devices with their start and end apart: 8, of which 6 were waited for; matrix products, arithmetic and copies ran while one was open for 0% of the time, Pallas kernels for 0%

commit v1 on v0

--- a/solution.py
+++ b/solution.py
@@ -95,7 +95,20 @@
             - 0.2 * jax.nn.sigmoid(cond[3]) * (temp - 0.5)
         )
         table = jnp.stack([rho_c, temp_c])[None]
-        whole = lax.all_gather(table, ("sec", "span"), axis=0, tiled=True)
+
+        def track_ends(xin, dim_k):
+            row_out = jnp.concatenate(
+                lax.all_to_all(
+                    jnp.stack(lax.axis_size(("sec", "span")) * [xin], axis=0),
+                    axis_name=("sec", "span"),
+                    split_axis=0,
+                    concat_axis=0,
+                ),
+                axis=dim_k,
+            )
+            return row_out
+
+        whole = track_ends(table, dim_k=0)
         rho_cell = whole[:, 0, :].reshape(-1)[index]
         temp_cell = whole[:, 1, :].reshape(-1)[index]
         extended = extended_2(fields, (("span", 2),), 1)

time: 1920 us -> 730 us (0.38)
  blocking collectives: 1250 us -> 0 us
  waiting for transfers between devices: 490 us -> 518 us
  starting transfers between devices: 11.1 us -> 36.3 us
    all_gather x2 -> x0, blocking collectives: 1250 us -> none  [body(): whole = lax.all_gather(table, ('sec', 'span'), axis=0, tiled=True)]
    all_to_all x0 -> x2, starting transfers between devices: none -> 22.8 us  [track_ends(): lax.all_to_all(jnp.stack(lax.axis_size(('sec', 'span')) * [xin], axis=0),...]
  transfers between devices with their start and end apart: 8 -> 10, of which waited for: 6 -> 6; matrix products, arithmetic and copies ran while one was open for 0% -> 1% of each run, Pallas kernels for 0% -> 0%
where the time goes in v1:
time: 730 us; the launch traced here: 726 us
  waiting for transfers between devices  518 us (71%)
  local copies, waits for them, and re-layouts  146 us (20%)
  starting transfers between devices  36.3 us (5%)
  between operations  14.4 us (2%)
  matrix products  7.84 us (1%)
    psum x2, waiting for transfers between devices, body(): lax.psum(lax.dot_general(hot, hist, (((0,), (0,)), ((), ())), precision=l...  494 us
    gather x3, local copies, waits for them, and re-layouts, body(): rho_cell = whole[:, 0, :].reshape(-1)[index]  69.2 us
    gather x4, local copies, waits for them, and re-layouts, body(): temp_cell = whole[:, 1, :].reshape(-1)[index]  68.6 us
    all_to_all x2, starting transfers between devices, track_ends(): lax.all_to_all(jnp.stack(lax.axis_size(('sec', 'span')) * [xin], axis=0),...  22.8 us
    all_to_all x2, waiting for transfers between devices, track_ends(): lax.all_to_all(jnp.stack(lax.axis_size(('sec', 'span')) * [xin], axis=0),...  17.8 us
  transfers between devices with their start and end apart: 10, of which 6 were waited for; matrix products, arithmetic and copies ran while one was open for 1% of the time, Pallas kernels for 0%

profile of v1, /device:TPU:0, one launch (start us, length us, event | category | flops | bytes accessed | tf_op | source)
XLA Modules:
  0.0 726.4 jit_solution(18070996482716206167)
XLA Ops:
  7.2 0.8 stack.44
  8.1 0.8 bitcast_multiply_fusion
  10.0 2.4 while.22
  11.6 0.8 fusion.68
  13.1 1.4 fusion.21
  15.2 1.8 collective-permute-start
  17.0 5.3 collective-permute-start.1
  22.4 248.3 %all-reduce.5.cloned.1.call-done = f32[256,640]{1,0:T(8,128)} async-done(((f32[256,640]{1,0:T(8,128)}), f32[256,640]{1,0:T(8,128)}) %all-reduce.5.cloned.1.call-update) | async-done | bytes 655376 | tf_op jit(solution)/shard_map/psum | solution.py:55
  273.9 11.4 %all-to-all-start = ((f32[256,1,2,128]{3,2,1,0:T(2,128)}), f32[256,1,2,128]{3,2,1,0:T(2,128)S(1)}, u32[]{:S(2)}, u32[]{:S(2)}) async-start(f32[256,1,2,128]{3,2,1,0:T(2,128)} %stack.51), calls=%async_computation | async-start | bytes 524288 | tf_op jit(solution)/shard_map/all_to_all | solution.py:101
  285.6 13.9 %all-to-all-done = f32[256,1,2,128]{3,2,1,0:T(2,128)S(1)} async-done(((f32[256,1,2,128]{3,2,1,0:T(2,128)}), f32[256,1,2,128]{3,2,1,0:T(2,128)S(1)}, u32[]{:S(2)}, u32[]{:S(2)}) %all-to-all-start) | async-done | bytes 262176 | tf_op jit(solution)/shard_map/all_to_all | solution.py:101
  299.8 34.3 %gather_fusion.1 = f32[6144]{0:T(1024)S(1)} fusion(f32[32768]{0:T(1024)S(1)} %bitcast.130, s32[6144]{0:T(1024)S(1)} %broadcast_clamp_fusion), kind=kCustom, calls=%fused_computation.1 | custom fusion | bytes 73728 | tf_op jit(solution)/shard_map/gather | solution.py:113
  334.1 34.3 %gather_fusion = f32[6144]{0:T(1024)S(1)} fusion(f32[32768]{0:T(1024)S(1)} %bitcast.128, s32[6144]{0:T(1024)S(1)} %broadcast_clamp_fusion), kind=kCustom, calls=%fused_computation | custom fusion | bytes 73728 | tf_op jit(solution)/shard_map/gather | solution.py:112
  368.7 2.5 while.23
  368.8 0.8 fusion.70
  371.2 1.4 fusion.18
  372.6 2.5 collective-permute-start.3
  375.2 245.5 %all-reduce.7.cloned.1.call-done = f32[256,640]{1,0:T(8,128)} async-done(((f32[256,640]{1,0:T(8,128)}), f32[256,640]{1,0:T(8,128)}) %all-reduce.7.cloned.1.call-update) | async-done | bytes 655376 | tf_op jit(solution)/shard_map/psum | solution.py:55
  623.8 11.4 %all-to-all-start.1 = ((f32[256,1,2,128]{3,2,1,0:T(2,128)}), f32[256,1,2,128]{3,2,1,0:T(2,128)S(1)}, u32[]{:S(2)}, u32[]{:S(2)}) async-start(f32[256,1,2,128]{3,2,1,0:T(2,128)} %stack.55), calls=%async_computation.1 | async-start | bytes 524288 | tf_op jit(solution)/shard_map/all_to_all | solution.py:101
  635.3 3.8 collective-permute-start.4
  639.1 1.7 collective-permute-done.4
  640.9 4.6 collective-permute-done.5
  645.6 3.9 all-to-all-done.1
  649.7 34.3 %gather_fusion.3 = f32[6144]{0:T(1024)S(1)} fusion(f32[32768]{0:T(1024)S(1)} %bitcast.131, s32[6144]{0:T(1024)S(1)} %broadcast_clamp_fusion), kind=kCustom, calls=%fused_computation.3 | custom fusion | bytes 73728 | tf_op jit(solution)/shard_map/gather | solution.py:113
  684.0 34.3 %gather_fusion.2 = f32[6144]{0:T(1024)S(1)} fusion(f32[32768]{0:T(1024)S(1)} %bitcast.129, s32[6144]{0:T(1024)S(1)} %broadcast_clamp_fusion), kind=kCustom, calls=%fused_computation.2 | custom fusion | bytes 73728 | tf_op jit(solution)/shard_map/gather | solution.py:112
  (80 shorter events, 14.5 us)
Async XLA Ops:
  7.2 265.1 %copy-start = (f32[32,32]{1,0:T(8,128)S(1)}, f32[32,32]{1,0:T(8,128)}, u32[]{:S(2)}) copy-start(f32[32,32]{1,0:T(8,128)} %param.21) | copy-start | bytes 12292
  7.2 263.5 %all-reduce.5.cloned.1.call-start = ((), (), s32[]{:S(2)}) async-start(), calls=%async_computation.2 | async-start | bytes 1310720 | tf_op jit(solution)/shard_map/psum | solution.py:55
  7.2 0.8 copy-start.4
  9.2 0.7 copy-start.2
  12.4 0.7 copy-start.5
  14.5 0.7 copy-start.7
  14.5 2.5 copy-start.1
  15.2 257.0 %collective-permute-start = (f32[1,32,128]{2,1,0:T(8,128)S(1)}, f32[1,32,128]{2,1,0:T(8,128)S(1)}, u32[]{:S(2)}, u32[]{:S(2)}) collective-permute-start(f32[1,32,128]{2,1,0:T(8,128)S(1)} %copy-done.7), channel_id=1, source_target_pairs={{0,1},{1,2},{2,3},{3,4},{4,5},{5,6},{6,7},{7,8},{8,9},{9,10},{10,1... | collective-permute-start | bytes 49160 | tf_op jit(solution)/shard_map/ppermute | solution.py:13
  17.0 268.4 %collective-permute-start.1 = (f32[4,24,1]{2,1,0:T(8,128)S(1)}, f32[4,24,1]{2,1,0:T(8,128)S(1)}, u32[]{:S(2)}, u32[]{:S(2)}) collective-permute-start(f32[4,24,1]{2,1,0:T(8,128)S(1)} %get-tuple-element.108), channel_id=1, source_target_pairs={{1,0},{2,1},{3,2},{4,3},{5,4},{6,5},{7,6},{8,7},{9,8},{10,9},{11,1... | collective-permute-start | bytes 1160 | tf_op jit(solution)/shard_map/ppermute | solution.py:24
  22.4 263.1 %collective-permute-start.2 = (f32[4,24,1]{2,1,0:T(8,128)S(1)}, f32[4,24,1]{2,1,0:T(8,128)S(1)}, u32[]{:S(2)}, u32[]{:S(2)}) collective-permute-start(f32[4,24,1]{2,1,0:T(8,128)S(1)} %get-tuple-element.109), channel_id=1, source_target_pairs={{0,1},{1,2},{2,3},{3,4},{4,5},{5,6},{6,7},{7,8},{8,9},{9,10},{10,1... | collective-permute-start | bytes 1160 | tf_op jit(solution)/shard_map/ppermute | solution.py:23
  272.2 0.7 copy-start.6
  272.2 0.7 copy-start.8
  273.9 25.7 %all-to-all-start = ((f32[256,1,2,128]{3,2,1,0:T(2,128)}), f32[256,1,2,128]{3,2,1,0:T(2,128)S(1)}, u32[]{:S(2)}, u32[]{:S(2)}) async-start(f32[256,1,2,128]{3,2,1,0:T(2,128)} %stack.51), calls=%async_computation | async-start | bytes 524288 | tf_op jit(solution)/shard_map/all_to_all | solution.py:101
  285.3 335.3 %all-reduce.7.cloned.1.call-start = ((), (), s32[]{:S(2)}) async-start(), calls=%async_computation.3 | async-start | bytes 1310720 | tf_op jit(solution)/shard_map/psum | solution.py:55
  372.6 249.7 %collective-permute-start.3 = (f32[1,32,128]{2,1,0:T(8,128)S(1)}, f32[1,32,128]{2,1,0:T(8,128)S(1)}, u32[]{:S(2)}, u32[]{:S(2)}) collective-permute-start(f32[1,32,128]{2,1,0:T(8,128)S(1)} %bitcast.139), channel_id=1, source_target_pairs={{0,1},{1,2},{2,3},{3,4},{4,5},{5,6},{6,7},{7,8},{8,9},{9,10},{10,1... | collective-permute-start | bytes 49160 | tf_op jit(solution)/shard_map/ppermute | solution.py:13
  623.8 25.7 %all-to-all-start.1 = ((f32[256,1,2,128]{3,2,1,0:T(2,128)}), f32[256,1,2,128]{3,2,1,0:T(2,128)S(1)}, u32[]{:S(2)}, u32[]{:S(2)}) async-start(f32[256,1,2,128]{3,2,1,0:T(2,128)} %stack.55), calls=%async_computation.1 | async-start | bytes 524288 | tf_op jit(solution)/shard_map/all_to_all | solution.py:101
  635.3 5.6 collective-permute-start.4
  639.1 6.4 collective-permute-start.5
  718.9 0.6 copy-start.3
Sparse Core Ops, SparseCore 0:
  14.6 256.0 all-reduce.4
  372.8 247.8 all-reduce.6
